TPU v7x, 32 devices: a whole 2x2x4 slice. The times are simulated.
32 devices in a mesh: dp: 2 (over x), expert: 16 (over z, y, core).
Axes of the slice: x: 2, y: 2, z: 4, core: 2. Of those that a mesh axis runs over, the one named last changes fastest.
Arguments:
- tokens: bfloat16 [4096, 1024], P(('dp', 'expert')), may hold values from -6 to 6
- cotangent: bfloat16 [4096, 1024], P(('dp', 'expert')), may hold values from -6 to 6
- expert_ids: int32 [4096, 6], P(('dp', 'expert')), may hold values from 0 to 15, all different within a row; in each aligned block of 128 rows (0 to 127, 128 to 255, ...) at most 60 rows name the same one
- gate_weights: float32 [4096, 6], P(('dp', 'expert')), may hold values from 0.05 to 0.3
- partner: int32 [16], replicated, may hold values from 0 to 15, as said below
- weights: bfloat16 [16, 1024, 3, 384], P('expert', 'dp'), may hold values from -0.3125 to 0.3125
- first_moment: bfloat16 [16, 1024, 3, 384], P('expert', 'dp'), may hold values from -6 to 6
- second_moment: bfloat16 [16, 1024, 3, 384], P('expert', 'dp'), may hold values from 0.099609375 to 4
Outputs:
- mixed: bfloat16 [4096, 1024], P(('dp', 'expert'))
- token_grad: bfloat16 [4096, 1024], P(('dp', 'expert'))
- new_weights: bfloat16 [16, 1024, 3, 384], P('expert', 'dp')
- new_first: bfloat16 [16, 1024, 3, 384], P('expert', 'dp')
- new_second: bfloat16 [16, 1024, 3, 384], P('expert', 'dp')
Inputs may be any that keep to these rules, and one draw needn't show every extreme that they name: `expert_ids`: each row names 6 different experts. Among the 128 tokens of one device (aligned blocks of rows), no expert is named by more than 60 tokens, and in every draw some block names some expert exactly 60 times. partner[partner[h]] = h and partner[h] != h for every h.
All inputs are finite; a program needn't handle non-finite values.
Results may differ from a plain program's by a relative error of at most 0.024.
Values may be sent and summed in bfloat16 or wider, within the bound.
A program may use at most 64 MiB of HBM per device.

v0:
```python
import jax
import jax.numpy as jnp
from jax import lax
from jax.sharding import PartitionSpec as P

beta_one = 0.9
beta_two = 0.95
learn_rate = 0.01
decay_rate = 0.1
eps_adam = 1e-08
step_count = 100


def send_rows(parts):
    return (lax.all_to_all(parts[0], "expert", split_axis=0, concat_axis=0, tiled=True),)


def send_back(parts):
    return (lax.all_to_all(parts[0], "expert", split_axis=0, concat_axis=0, tiled=True),)


def shards_by_slot(
    tokens, cotangent, expert_ids, gate_weights, partner, weights, first_moment, second_moment
):
    experts_here = lax.axis_size("expert")
    tok_dev, model_width = tokens.shape
    top_count = expert_ids.shape[1]
    hidden_width = weights.shape[3]
    capacity = min(tok_dev, max(2, 5 * tok_dev * top_count // (4 * experts_here)))
    item_total = tok_dev * top_count
    slot_total = experts_here * capacity
    flat_ids = expert_ids.reshape(item_total)
    onehot = (flat_ids[:, None] == jnp.arange(experts_here, dtype=jnp.int32)[None, :]).astype(
        jnp.int32
    )
    before = jnp.cumsum(onehot, axis=0) - onehot
    slot_of = jnp.sum(before * onehot, axis=1)
    position = flat_ids * capacity + slot_of
    source = (
        jnp.full((slot_total,), item_total, jnp.int32)
        .at[position]
        .set(jnp.arange(item_total, dtype=jnp.int32))
    )
    token_of = source // top_count
    zero_row = jnp.zeros((1, model_width), jnp.bfloat16)
    x_send = jnp.concatenate([tokens, zero_row], axis=0)[token_of].reshape(
        experts_here, capacity, model_width
    )
    gate_flat = gate_weights.reshape(item_total)
    gate_pad = jnp.concatenate([gate_flat, jnp.zeros((1,), jnp.float32)])
    cot_rows = jnp.concatenate([cotangent, zero_row], axis=0)[token_of].astype(jnp.float32)
    dy_send = (
        (gate_pad[source][:, None] * cot_rows)
        .astype(jnp.bfloat16)
        .reshape(experts_here, capacity, model_width)
    )
    gathered = lax.all_gather(weights, "dp", axis=1, tiled=True)[0]
    gate_up = gathered[:, 0:2, :].reshape(model_width, 2 * hidden_width)
    down_proj = gathered[:, 2, :]
    block_shape = (experts_here, capacity, model_width)
    (x_recv,) = send_rows((x_send,))
    forward_x_rows = x_recv.reshape(slot_total, model_width)
    both_proj = jnp.dot(forward_x_rows, gate_up, preferred_element_type=jnp.float32)
    pre_act = both_proj[:, :hidden_width]
    lin_act = both_proj[:, hidden_width:]
    sigmoid_pre = jax.nn.sigmoid(pre_act)
    silu_pre = pre_act * sigmoid_pre
    forward_hidden = (silu_pre * lin_act).astype(jnp.bfloat16)
    out_rows = jnp.dot(forward_hidden, down_proj.T, preferred_element_type=jnp.float32).astype(
        jnp.bfloat16
    )
    x_rows, saved, hidden, out_rows = (
        forward_x_rows,
        (pre_act, lin_act, sigmoid_pre, silu_pre),
        forward_hidden,
        out_rows,
    )
    (out_back,) = send_back((out_rows.reshape(block_shape),))
    (dy_recv,) = send_rows((dy_send,))
    pre_act, lin_act, sigmoid_pre, silu_pre = saved
    backward_dy_rows = dy_recv.reshape(slot_total, model_width)
    hidden_grad = jnp.dot(backward_dy_rows, down_proj, preferred_element_type=jnp.float32)
    pre_grad = (hidden_grad * lin_act * sigmoid_pre * (1.0 + pre_act * (1.0 - sigmoid_pre))).astype(
        jnp.bfloat16
    )
    lin_grad = (hidden_grad * silu_pre).astype(jnp.bfloat16)
    backward_both_grad = jnp.concatenate([pre_grad, lin_grad], axis=1)
    item_grad = jnp.dot(backward_both_grad, gate_up.T, preferred_element_type=jnp.float32).astype(
        jnp.bfloat16
    )
    dy_rows, both_grad, item_grad = (backward_dy_rows, backward_both_grad, item_grad)
    (grad_back,) = send_back((item_grad.reshape(block_shape),))
    out_items = (
        out_back.reshape(slot_total, model_width)[position].astype(jnp.float32) * gate_flat[:, None]
    )
    mixed = jnp.sum(out_items.reshape(tok_dev, top_count, model_width), axis=1).astype(jnp.bfloat16)
    grad_items = grad_back.reshape(slot_total, model_width)[position].astype(jnp.float32)
    token_grad = jnp.sum(grad_items.reshape(tok_dev, top_count, model_width), axis=1).astype(
        jnp.bfloat16
    )
    count = lax.axis_size("dp") * weights.shape[1]
    proj_grad = jnp.dot(x_rows.T, both_grad, preferred_element_type=jnp.float32)
    down_grad = jnp.dot(dy_rows.T, hidden, preferred_element_type=jnp.float32)
    grad_sum = lax.psum_scatter(
        jnp.concatenate(
            [proj_grad.reshape(count, 2, hidden_width), down_grad.reshape(count, 1, hidden_width)],
            axis=1,
        ).astype(jnp.bfloat16),
        "dp",
        scatter_dimension=0,
        tiled=True,
    ).astype(jnp.float32)
    w_old = weights[0].astype(jnp.float32)
    m_old = first_moment[0].astype(jnp.float32)
    v_old = second_moment[0].astype(jnp.float32)
    m_new = beta_one * m_old + (1.0 - beta_one) * grad_sum
    v_new = beta_two * v_old + (1.0 - beta_two) * grad_sum * grad_sum
    m_hat = m_new / (1.0 - beta_one**step_count)
    v_hat = v_new / (1.0 - beta_two**step_count)
    w_new = w_old - learn_rate * (m_hat / (jnp.sqrt(v_hat) + eps_adam) + decay_rate * w_old)
    pieces = (
        w_new.astype(jnp.bfloat16).reshape(experts_here, -1),
        m_new.astype(jnp.bfloat16).reshape(experts_here, -1),
        v_new.astype(jnp.bfloat16).reshape(experts_here, -1),
    )
    spread = (
        lax.all_to_all(pieces[0], "expert", split_axis=0, concat_axis=0, tiled=True),
        lax.all_to_all(pieces[1], "expert", split_axis=0, concat_axis=0, tiled=True),
        lax.all_to_all(pieces[2], "expert", split_axis=0, concat_axis=0, tiled=True),
    )
    ordered = (spread[0][partner], spread[1][partner], spread[2][partner])
    homed = (
        lax.all_to_all(ordered[0], "expert", split_axis=0, concat_axis=0, tiled=True),
        lax.all_to_all(ordered[1], "expert", split_axis=0, concat_axis=0, tiled=True),
        lax.all_to_all(ordered[2], "expert", split_axis=0, concat_axis=0, tiled=True),
    )
    new_weights = homed[0].reshape(weights.shape)
    new_first = homed[1].reshape(weights.shape)
    new_second = homed[2].reshape(weights.shape)
    return (mixed, token_grad, new_weights, new_first, new_second)


def adam(w_old, m_old, v_old, grad_sum):
    m_new = beta_one * m_old + (1.0 - beta_one) * grad_sum
    v_new = beta_two * v_old + (1.0 - beta_two) * grad_sum * grad_sum
    m_hat = m_new / (1.0 - beta_one**step_count)
    v_hat = v_new / (1.0 - beta_two**step_count)
    w_new = w_old - learn_rate * (m_hat / (jnp.sqrt(v_hat) + eps_adam) + decay_rate * w_old)
    return (w_new, m_new, v_new)


def shards_dense(
    tokens, cotangent, expert_ids, gate_weights, partner, weights, first_moment, second_moment
):
    experts_here = lax.axis_size("expert")
    me = lax.axis_index("expert")
    tok_dev, model_width = tokens.shape
    own_rows, hidden_width = (weights.shape[1], weights.shape[3])
    width = 3 * hidden_width
    f32, bf16 = (jnp.float32, jnp.bfloat16)
    hits = expert_ids[:, :, None] == jnp.arange(experts_here, dtype=jnp.int32)[None, None, :]
    gate_table = jnp.sum(jnp.where(hits, gate_weights[:, :, None], 0.0), axis=1).T
    w_flat = weights[0].reshape(own_rows, width)
    gathered = lax.all_gather(w_flat, "dp", axis=0, tiled=True)
    x_rows = lax.all_gather(tokens, "expert", axis=0, tiled=True)
    cot_rows = lax.all_gather(cotangent, "expert", axis=0, tiled=True)
    gate_all = lax.all_gather(gate_table, "expert", axis=0)
    gate = lax.dynamic_index_in_dim(gate_all, me, 1, keepdims=False)
    gate = gate.reshape(experts_here * tok_dev, 1)
    gate_up = gathered[:, : 2 * hidden_width]
    down_proj = gathered[:, 2 * hidden_width :]
    both_proj = jnp.dot(x_rows, gate_up, preferred_element_type=f32)
    pre_act = both_proj[:, :hidden_width]
    lin_act = both_proj[:, hidden_width:]
    sigmoid_pre = jax.nn.sigmoid(pre_act)
    silu_pre = pre_act * sigmoid_pre
    hidden = (silu_pre * lin_act).astype(bf16)
    out_rows = jnp.dot(hidden, down_proj.T, preferred_element_type=f32)
    mixed = lax.psum_scatter(
        (gate * out_rows).astype(bf16), "expert", scatter_dimension=0, tiled=True
    )
    dy_rows = (gate * cot_rows.astype(f32)).astype(bf16)
    hidden_grad = jnp.dot(dy_rows, down_proj, preferred_element_type=f32)
    pre_grad = hidden_grad * lin_act * sigmoid_pre * (1.0 + pre_act * (1.0 - sigmoid_pre))
    lin_grad = hidden_grad * silu_pre
    both_grad = jnp.concatenate([pre_grad.astype(bf16), lin_grad.astype(bf16)], axis=1)
    proj_grad = jnp.dot(x_rows.T, both_grad, preferred_element_type=f32)
    down_grad = jnp.dot(dy_rows.T, hidden, preferred_element_type=f32)
    partial = jnp.concatenate([proj_grad.astype(bf16), down_grad.astype(bf16)], axis=1)
    grad_sum = lax.psum_scatter(partial, "dp", scatter_dimension=0, tiled=True).astype(f32)
    item_grad = jnp.dot(both_grad, gate_up.T, preferred_element_type=f32).astype(bf16)
    token_grad = lax.psum_scatter(item_grad, "expert", scatter_dimension=0, tiled=True)
    m_flat = first_moment[0].reshape(own_rows, width)
    v_flat = second_moment[0].reshape(own_rows, width)
    new_state = adam(w_flat.astype(f32), m_flat.astype(f32), v_flat.astype(f32), grad_sum)
    share = own_rows // experts_here
    outs = []
    for part in new_state:
        pieces = part.astype(bf16).reshape(experts_here, share, width)
        spread = lax.all_to_all(pieces, "expert", split_axis=0, concat_axis=0, tiled=True)
        homed = lax.all_to_all(spread[partner], "expert", split_axis=0, concat_axis=0, tiled=True)
        outs.append(homed.reshape(weights.shape))
    return (mixed, token_grad, *outs)


def shards(*args):
    replica_rows = lax.axis_size("expert") * args[0].shape[0]
    if replica_rows <= 4096 and args[5].shape[1] % (16 * lax.axis_size("expert")) == 0:
        return shards_dense(*args)
    return shards_by_slot(*args)


def solution(mesh):
    in_specs = (
        P(("dp", "expert"), None),
        P(("dp", "expert"), None),
        P(("dp", "expert"), None),
        P(("dp", "expert"), None),
        P(),
        P("expert", "dp", None, None),
        P("expert", "dp", None, None),
        P("expert", "dp", None, None),
    )
    out_specs = (
        P(("dp", "expert"), None),
        P(("dp", "expert"), None),
        P("expert", "dp", None, None),
        P("expert", "dp", None, None),
        P("expert", "dp", None, None),
    )
    return jax.shard_map(shards, mesh=mesh, in_specs=in_specs, out_specs=out_specs, check_vma=False)
```

profile of v0, /device:TPU:15, one launch (start us, length us, event | category | flops | bytes accessed | tf_op | source)
XLA Modules:
  0.0 465.4 jit_solution(3843170583067933573)
XLA Ops:
  7.2 2.4 copy.29
  11.2 16.0 %all-gather = f32[256,128]{1,0:T(8,128)S(1)} all-gather(f32[16,128]{1,0:T(8,128)S(1)} %bitcast.29), channel_id=2, replica_groups=mesh['dp'=2,'expert'=16] {'expert'}, dimensions={0}, use_global_device_ids=true | all-gather | bytes 139264 | tf_op jit(solution)/shard_map/all_gather | solution.py:167
  27.2 19.2 %all-gather.7.cloned.1.call-done = bf16[1024,1152]{0,1:T(8,128)(2,1)} async-done(((bf16[512,1152]{0,1:T(8,128)(2,1)}), bf16[1024,1152]{0,1:T(8,128)(2,1)}) %all-gather.7.cloned.1.call-update) | async-done | bytes 2359312 | tf_op jit(solution)/shard_map/all_gather | solution.py:164
  46.4 53.2 %all-gather.5.cloned.1.call-done = bf16[2048,1024]{1,0:T(8,128)(2,1)} async-done(((bf16[128,1024]{1,0:T(8,128)(2,1)}), bf16[2048,1024]{1,0:T(8,128)(2,1)}) %all-gather.5.cloned.1.call-update) | async-done | bytes 4194320 | tf_op jit(solution)/shard_map/all_gather | solution.py:165
  99.6 8.7 %fusion.14 = f32[2048,768]{0,1:T(8,128)} fusion(bf16[2048,1024]{1,0:T(8,128)(2,1)} %all-gather.5.cloned.1.call-done, bf16[1024,1152]{0,1:T(8,128)(2,1)} %all-gather.7.cloned.1.call-done), kind=kOutput, calls=%fused_computation.32 | convolution fusion | flops 3221225472 | bytes 12058624 | tf_op jit(solution)/shard_map/dot_general | solution.py:172
  108.4 42.5 %all-gather.9.cloned.1.call-done = bf16[2048,1024]{1,0:T(8,128)(2,1)} async-done(((bf16[128,1024]{1,0:T(8,128)(2,1)}), bf16[2048,1024]{1,0:T(8,128)(2,1)}) %all-gather.9.cloned.1.call-update) | async-done | bytes 4194320 | tf_op jit(solution)/shard_map/all_gather | solution.py:166
  150.9 7.5 %multiply_convert_fusion.3 = (bf16[2048,384]{0,1:T(8,128)(2,1)S(1)}, bf16[2048,384]{0,1:T(8,128)(2,1)S(1)}, bf16[2048,384]{0,1:T(8,128)(2,1)S(1)}) fusion(f32[2048,768]{0,1:T(8,128)} %fusion.14, bf16[1024,1152]{0,1:T(8,128)(2,1)} %all-gather.7.cloned.1.call-done, bf16[2048,1024]{1,0:T(8,128)(2,1)} %all-gather.9.cloned.1.call-done, f32[2048]{0:T(1024)S(1)} %bitcast.30), kind=kOutput, calls=%fused_computation.9 | convolution fusion | flops 1628700672 | bytes 15998976 | tf_op jit(solution)/shard_map/dot_general | solution.py:183
  162.2 3.4 fusion.10
  174.6 25.7 %reduce-scatter.8.cloned.1.call-done = bf16[512,1152]{0,1:T(8,128)(2,1)} async-done(((bf16[1024,1152]{0,1:T(8,128)(2,1)}), bf16[512,1152]{0,1:T(8,128)(2,1)}) %reduce-scatter.8.cloned.1.call-update) | async-done | bytes 1179664 | tf_op jit(solution)/shard_map/reduce_scatter | solution.py:190
  200.3 5.8 %fusion.16 = (bf16[512,1152]{0,1:T(8,128)(2,1)S(1)}, bf16[512,1152]{0,1:T(8,128)(2,1)}, bf16[512,1152]{0,1:T(8,128)(2,1)S(1)}) fusion(bf16[512,1152]{0,1:T(8,128)(2,1)} %reduce-scatter.8.cloned.1.call-done, f32[1,512,3,384]{1,3,2,0:T(8,128)} %copy.31, f32[1,512,3,384]{1,3,2,0:T(8,128)} %copy.30, bf16[1,512,3,384]{1,3,2,0:T(8,128)(2,1)S(1)} %copy-done), kind=kLoop, calls=%fused_computation.34 | loop fusion | flops 10616832 | bytes 10616832 | tf_op jit(solution)/shard_map/convert_element_type | solution.py:199
  208.5 6.4 %all-to-all-start = ((bf16[16,32,1152]{2,1,0:T(8,128)(2,1)}), bf16[16,32,1152]{2,1,0:T(8,128)(2,1)S(1)}, u32[]{:S(2)}, u32[]{:S(2)}) async-start(bf16[16,32,1152]{2,1,0:T(8,128)(2,1)} %bitcast.7), calls=%async_computation.3 | async-start | bytes 2359296 | tf_op jit(solution)/shard_map/all_to_all | solution.py:200
  214.9 7.8 %convolution_convert_fusion = bf16[2048,1024]{1,0:T(8,128)(2,1)} fusion(bf16[2048,384]{0,1:T(8,128)(2,1)} %copy-done.11, bf16[2048,384]{0,1:T(8,128)(2,1)} %copy-done.10, bf16[1024,1152]{0,1:T(8,128)(2,1)} %all-gather.7.cloned.1.call-done), kind=kOutput, calls=%fused_computation.5 | convolution fusion | flops 3229614080 | bytes 8912896 | tf_op jit(solution)/shard_map/dot_general | solution.py:191
  224.1 18.5 %all-to-all-done = bf16[16,32,1152]{2,1,0:T(8,128)(2,1)S(1)} async-done(((bf16[16,32,1152]{2,1,0:T(8,128)(2,1)}), bf16[16,32,1152]{2,1,0:T(8,128)(2,1)S(1)}, u32[]{:S(2)}, u32[]{:S(2)}) %all-to-all-start) | async-done | bytes 1179680 | tf_op jit(solution)/shard_map/all_to_all | solution.py:200
  242.6 4.9 %all-to-all-start.2 = ((bf16[16,32,1152]{2,1,0:T(8,128)(2,1)}), bf16[16,32,1152]{2,1,0:T(8,128)(2,1)S(1)}, u32[]{:S(2)}, u32[]{:S(2)}) async-start(bf16[16,32,1152]{2,1,0:T(8,128)(2,1)} %bitcast.8), calls=%async_computation.5 | async-start | bytes 2359296 | tf_op jit(solution)/shard_map/all_to_all | solution.py:200
  248.9 43.1 %all-to-all-done.2 = bf16[16,32,1152]{2,1,0:T(8,128)(2,1)S(1)} async-done(((bf16[16,32,1152]{2,1,0:T(8,128)(2,1)}), bf16[16,32,1152]{2,1,0:T(8,128)(2,1)S(1)}, u32[]{:S(2)}, u32[]{:S(2)}) %all-to-all-start.2) | async-done | bytes 1179680 | tf_op jit(solution)/shard_map/all_to_all | solution.py:200
  292.1 4.9 %all-to-all-start.4 = ((bf16[16,32,1152]{2,1,0:T(8,128)(2,1)}), bf16[16,32,1152]{2,1,0:T(8,128)(2,1)S(1)}, u32[]{:S(2)}, u32[]{:S(2)}) async-start(bf16[16,32,1152]{2,1,0:T(8,128)(2,1)} %bitcast.27), calls=%async_computation.7 | async-start | bytes 2359296 | tf_op jit(solution)/shard_map/all_to_all | solution.py:200
  298.6 33.8 %all-to-all-done.4 = bf16[16,32,1152]{2,1,0:T(8,128)(2,1)S(1)} async-done(((bf16[16,32,1152]{2,1,0:T(8,128)(2,1)}), bf16[16,32,1152]{2,1,0:T(8,128)(2,1)S(1)}, u32[]{:S(2)}, u32[]{:S(2)}) %all-to-all-start.4) | async-done | bytes 1179680 | tf_op jit(solution)/shard_map/all_to_all | solution.py:200
  332.4 5.1 %all-to-all-start.1 = ((bf16[16,32,1152]{2,1,0:T(8,128)(2,1)}), bf16[16,32,1152]{2,1,0:T(8,128)(2,1)S(1)}, u32[]{:S(2)}, u32[]{:S(2)}) async-start(bf16[16,32,1152]{2,1,0:T(8,128)(2,1)} %gather_fusion), calls=%async_computation.4 | async-start | bytes 2359296 | tf_op jit(solution)/shard_map/all_to_all | solution.py:201
  337.5 6.0 %multiply_convert_fusion.1 = bf16[2048,1024]{1,0:T(8,128)(2,1)} fusion(bf16[2048,384]{0,1:T(8,128)(2,1)} %copy-done.9, f32[2048]{0:T(1024)S(1)} %bitcast.32, bf16[1024,1152]{0,1:T(8,128)(2,1)} %all-gather.7.cloned.1.call-done), kind=kOutput, calls=%fused_computation.4 | convolution fusion | flops 1614807040 | bytes 6561792 | tf_op jit(solution)/shard_map/dot_general | solution.py:178
  345.2 20.0 %all-to-all-done.1 = bf16[16,32,1152]{2,1,0:T(8,128)(2,1)S(1)} async-done(((bf16[16,32,1152]{2,1,0:T(8,128)(2,1)}), bf16[16,32,1152]{2,1,0:T(8,128)(2,1)S(1)}, u32[]{:S(2)}, u32[]{:S(2)}) %all-to-all-start.1) | async-done | bytes 1179680 | tf_op jit(solution)/shard_map/all_to_all | solution.py:201
  365.2 4.9 %all-to-all-start.3 = ((bf16[16,32,1152]{2,1,0:T(8,128)(2,1)}), bf16[16,32,1152]{2,1,0:T(8,128)(2,1)}, u32[]{:S(2)}, u32[]{:S(2)}) async-start(bf16[16,32,1152]{2,1,0:T(8,128)(2,1)} %gather_fusion.1), calls=%async_computation.6 | async-start | bytes 2359296 | tf_op jit(solution)/shard_map/all_to_all | solution.py:201
  371.8 43.0 %all-to-all-done.3 = bf16[16,32,1152]{2,1,0:T(8,128)(2,1)} async-done(((bf16[16,32,1152]{2,1,0:T(8,128)(2,1)}), bf16[16,32,1152]{2,1,0:T(8,128)(2,1)}, u32[]{:S(2)}, u32[]{:S(2)}) %all-to-all-start.3) | async-done | bytes 1179680 | tf_op jit(solution)/shard_map/all_to_all | solution.py:201
  414.8 5.0 %all-to-all-start.5 = ((bf16[16,32,1152]{2,1,0:T(8,128)(2,1)}), bf16[16,32,1152]{2,1,0:T(8,128)(2,1)}, u32[]{:S(2)}, u32[]{:S(2)}) async-start(bf16[16,32,1152]{2,1,0:T(8,128)(2,1)} %gather_fusion.2), calls=%async_computation.8 | async-start | bytes 2359296 | tf_op jit(solution)/shard_map/all_to_all | solution.py:201
  424.7 30.4 %all-to-all-done.5 = bf16[16,32,1152]{2,1,0:T(8,128)(2,1)} async-done(((bf16[16,32,1152]{2,1,0:T(8,128)(2,1)}), bf16[16,32,1152]{2,1,0:T(8,128)(2,1)}, u32[]{:S(2)}, u32[]{:S(2)}) %all-to-all-start.5) | async-done | bytes 1179680 | tf_op jit(solution)/shard_map/all_to_all | solution.py:201
  (60 shorter events, 33.0 us)
Async XLA Ops:
  7.2 4.0 copy-start.5
  7.2 4.0 copy-start.4
  7.2 39.2 %all-gather.7.cloned.1.call-start = ((), (), s32[]{:S(2)}) async-start(), calls=%async_computation.10 | async-start | bytes 3538944 | tf_op jit(solution)/shard_map/all_gather | solution.py:164
  9.6 90.0 %all-gather.5.cloned.1.call-start = ((), (), s32[]{:S(2)}) async-start(), calls=%async_computation.9 | async-start | bytes 4456448 | tf_op jit(solution)/shard_map/all_gather | solution.py:165
  10.4 140.5 %all-gather.9.cloned.1.call-start = ((), (), s32[]{:S(2)}) async-start(), calls=%async_computation.12 | async-start | bytes 4456448 | tf_op jit(solution)/shard_map/all_gather | solution.py:166
  11.1 189.2 %reduce-scatter.8.cloned.1.call-start = ((), (), s32[]{:S(2)}) async-start(), calls=%async_computation.14 | async-start | bytes 3538944 | tf_op jit(solution)/shard_map/reduce_scatter | solution.py:190
  150.9 7.5 %copy-start.7 = (bf16[2048,1024]{1,0:T(8,128)(2,1)S(1)}, bf16[2048,1024]{1,0:T(8,128)(2,1)}, u32[]{:S(2)}) copy-start(bf16[2048,1024]{1,0:T(8,128)(2,1)} %all-gather.9.cloned.1.call-done) | copy-start | bytes 12582916
  158.3 2.0 copy-start.9
  158.3 2.0 copy-start.10
  158.4 2.4 copy-start.11
  158.4 3.9 copy-start.6
  167.3 1.3 copy-start.3
  172.6 27.7 %copy-start = (bf16[1,512,3,384]{1,3,2,0:T(8,128)(2,1)S(1)}, bf16[1,512,3,384]{1,3,2,0:T(8,128)(2,1)}, u32[]{:S(2)}) copy-start(bf16[1,512,3,384]{1,3,2,0:T(8,128)(2,1)} %copy.29) | copy-start | bytes 3538948
  208.5 34.1 %all-to-all-start = ((bf16[16,32,1152]{2,1,0:T(8,128)(2,1)}), bf16[16,32,1152]{2,1,0:T(8,128)(2,1)S(1)}, u32[]{:S(2)}, u32[]{:S(2)}) async-start(bf16[16,32,1152]{2,1,0:T(8,128)(2,1)} %bitcast.7), calls=%async_computation.3 | async-start | bytes 2359296 | tf_op jit(solution)/shard_map/all_to_all | solution.py:200
  214.9 243.7 %reduce-scatter.6.cloned.1.call-start = ((), (), s32[]{:S(2)}) async-start(), calls=%async_computation.13 | async-start | bytes 4456448 | tf_op jit(solution)/shard_map/reduce_scatter | solution.py:192
  242.6 49.4 %all-to-all-start.2 = ((bf16[16,32,1152]{2,1,0:T(8,128)(2,1)}), bf16[16,32,1152]{2,1,0:T(8,128)(2,1)S(1)}, u32[]{:S(2)}, u32[]{:S(2)}) async-start(bf16[16,32,1152]{2,1,0:T(8,128)(2,1)} %bitcast.8), calls=%async_computation.5 | async-start | bytes 2359296 | tf_op jit(solution)/shard_map/all_to_all | solution.py:200
  247.5 49.4 %copy-start.8 = (s32[16]{0:T(128)S(1)}, s32[16]{0:T(128)}, u32[]{:S(2)}) copy-start(s32[16]{0:T(128)} %param.12) | copy-start | bytes 196
  292.1 40.4 %all-to-all-start.4 = ((bf16[16,32,1152]{2,1,0:T(8,128)(2,1)}), bf16[16,32,1152]{2,1,0:T(8,128)(2,1)S(1)}, u32[]{:S(2)}, u32[]{:S(2)}) async-start(bf16[16,32,1152]{2,1,0:T(8,128)(2,1)} %bitcast.27), calls=%async_computation.7 | async-start | bytes 2359296 | tf_op jit(solution)/shard_map/all_to_all | solution.py:200
  332.4 32.8 %all-to-all-start.1 = ((bf16[16,32,1152]{2,1,0:T(8,128)(2,1)}), bf16[16,32,1152]{2,1,0:T(8,128)(2,1)S(1)}, u32[]{:S(2)}, u32[]{:S(2)}) async-start(bf16[16,32,1152]{2,1,0:T(8,128)(2,1)} %gather_fusion), calls=%async_computation.4 | async-start | bytes 2359296 | tf_op jit(solution)/shard_map/all_to_all | solution.py:201
  337.5 121.1 %reduce-scatter.4.cloned.1.call-start = ((), (), s32[]{:S(2)}) async-start(), calls=%async_computation.11 | async-start | bytes 4456448 | tf_op jit(solution)/shard_map/reduce_scatter | solution.py:179
  365.2 6.6 %copy-start.1 = (bf16[16,32,1152]{2,1,0:T(8,128)(2,1)}, bf16[16,32,1152]{2,1,0:T(8,128)(2,1)S(1)}, u32[]{:S(2)}) copy-start(bf16[16,32,1152]{2,1,0:T(8,128)(2,1)S(1)} %all-to-all-done.1) | copy-start | bytes 3538948
  365.2 49.5 %all-to-all-start.3 = ((bf16[16,32,1152]{2,1,0:T(8,128)(2,1)}), bf16[16,32,1152]{2,1,0:T(8,128)(2,1)}, u32[]{:S(2)}, u32[]{:S(2)}) async-start(bf16[16,32,1152]{2,1,0:T(8,128)(2,1)} %gather_fusion.1), calls=%async_computation.6 | async-start | bytes 2359296 | tf_op jit(solution)/shard_map/all_to_all | solution.py:201
  414.8 5.0 %copy-start.2 = (bf16[16,32,1152]{2,1,0:T(8,128)(2,1)S(1)}, bf16[16,32,1152]{2,1,0:T(8,128)(2,1)}, u32[]{:S(2)}) copy-start(bf16[16,32,1152]{2,1,0:T(8,128)(2,1)} %copy-done.1) | copy-start | bytes 3538948
  414.8 40.4 %all-to-all-start.5 = ((bf16[16,32,1152]{2,1,0:T(8,128)(2,1)}), bf16[16,32,1152]{2,1,0:T(8,128)(2,1)}, u32[]{:S(2)}, u32[]{:S(2)}) async-start(bf16[16,32,1152]{2,1,0:T(8,128)(2,1)} %gather_fusion.2), calls=%async_computation.8 | async-start | bytes 2359296 | tf_op jit(solution)/shard_map/all_to_all | solution.py:201
Sparse Core Ops, SparseCore 0:
  10.1 36.2 all-gather.6
  48.6 50.9 all-gather.4
  101.8 49.0 all-gather.8
  167.5 32.7 reduce-scatter.7
  222.9 95.5 reduce-scatter.5
  343.7 96.6 reduce-scatter.3
where the time goes:
time: 466 us; the launch traced here: 465 us
  waiting for transfers between devices  331 us (71%)
  matrix products  35.4 us (8%)
  starting transfers between devices  31.2 us (7%)
  local copies, waits for them, and re-layouts  28.5 us (6%)
  blocking collectives  16 us (3%)
  between operations  14.3 us (3%)
  other arithmetic  9.17 us (2%)
    all_to_all x3, waiting for transfers between devices, shards_dense(): lax.all_to_all(pieces, 'expert', split_axis=0, concat_axis=0, tiled=True)  95.4 us
    all_to_all x3, waiting for transfers between devices, shards_dense(): lax.all_to_all(spread[partner], 'expert', split_axis=0, concat_axis=0, ti...  93.4 us
    all_gather x1, waiting for transfers between devices, shards_dense(): x_rows = lax.all_gather(tokens, 'expert', axis=0, tiled=True)  53.2 us
    all_gather x1, waiting for transfers between devices, shards_dense(): cot_rows = lax.all_gather(cotangent, 'expert', axis=0, tiled=True)  42.5 us
    reduce_scatter x1, waiting for transfers between devices, shards_dense(): lax.psum_scatter(partial, 'dp', scatter_dimension=0, tiled=True).astype(f32)  25.7 us
    all_gather x1, waiting for transfers between devices, shards_dense(): gathered = lax.all_gather(w_flat, 'dp', axis=0, tiled=True)  19.2 us
    all_to_all x3, starting transfers between devices, shards_dense(): lax.all_to_all(pieces, 'expert', split_axis=0, concat_axis=0, tiled=True)  16.1 us
    all_gather x1, blocking collectives, shards_dense(): gate_all = lax.all_gather(gate_table, 'expert', axis=0)  16 us
  transfers between devices with their start and end apart: 12, of which 10 were waited for; matrix products, arithmetic and copies ran while one was open for 10% of the time, Pallas kernels for 0%

commit v1 on v0

--- a/solution.py
+++ b/solution.py
@@ -162,8 +162,11 @@
     gate_table = jnp.sum(jnp.where(hits, gate_weights[:, :, None], 0.0), axis=1).T
     w_flat = weights[0].reshape(own_rows, width)
     gathered = lax.all_gather(w_flat, "dp", axis=0, tiled=True)
-    x_rows = lax.all_gather(tokens, "expert", axis=0, tiled=True)
-    cot_rows = lax.all_gather(cotangent, "expert", axis=0, tiled=True)
+    x_rows, cot_rows = jnp.split(
+        lax.all_gather(jnp.concatenate([tokens, cotangent], axis=1), "expert", axis=0, tiled=True),
+        [tokens.shape[1]],
+        axis=1,
+    )
     gate_all = lax.all_gather(gate_table, "expert", axis=0)
     gate = lax.dynamic_index_in_dim(gate_all, me, 1, keepdims=False)
     gate = gate.reshape(experts_here * tok_dev, 1)

time: 466 us -> 441 us (0.946)
  waiting for transfers between devices: 331 us -> 312 us
  matrix products: 35.4 us -> 29.8 us
    all_gather x2 -> x1, waiting for transfers between devices: 95.7 us -> 77.5 us  [shards_dense(): lax.all_gather(jnp.concatenate([tokens, cotangent], axis=1), 'expert', ax...]
  transfers between devices with their start and end apart: 12 -> 11, of which waited for: 10 -> 9; matrix products, arithmetic and copies ran while one was open for 10% -> 8% of each run, Pallas kernels for 0% -> 0%
where the time goes in v1:
time: 441 us; the launch traced here: 440 us
  waiting for transfers between devices  312 us (71%)
  starting transfers between devices  31.2 us (7%)
  matrix products  29.8 us (7%)
  local copies, waits for them, and re-layouts  26.6 us (6%)
  blocking collectives  16 us (4%)
  between operations  14 us (3%)
  other arithmetic  10 us (2%)
    all_to_all x3, waiting for transfers between devices, shards_dense(): lax.all_to_all(pieces, 'expert', split_axis=0, concat_axis=0, tiled=True)  95.4 us
    all_to_all x3, waiting for transfers between devices, shards_dense(): lax.all_to_all(spread[partner], 'expert', split_axis=0, concat_axis=0, ti...  93.4 us
    all_gather x1, waiting for transfers between devices, shards_dense(): lax.all_gather(jnp.concatenate([tokens, cotangent], axis=1), 'expert', ax...  77.5 us
    reduce_scatter x1, waiting for transfers between devices, shards_dense(): lax.psum_scatter(partial, 'dp', scatter_dimension=0, tiled=True).astype(f32)  26.2 us
    all_gather x1, waiting for transfers between devices, shards_dense(): gathered = lax.all_gather(w_flat, 'dp', axis=0, tiled=True)  19.7 us
    all_to_all x3, starting transfers between devices, shards_dense(): lax.all_to_all(pieces, 'expert', split_axis=0, concat_axis=0, tiled=True)  16.1 us
    all_gather x1, blocking collectives, shards_dense(): gate_all = lax.all_gather(gate_table, 'expert', axis=0)  16 us
    all_to_all x3, starting transfers between devices, shards_dense(): lax.all_to_all(spread[partner], 'expert', split_axis=0, concat_axis=0, ti...  14.9 us
  transfers between devices with their start and end apart: 11, of which 9 were waited for; matrix products, arithmetic and copies ran while one was open for 8% of the time, Pallas kernels for 0%

profile of v1, /device:TPU:15, one launch (start us, length us, event | category | flops | bytes accessed | tf_op | source)
XLA Modules:
  0.0 439.9 jit_solution(18377606548891000793)
XLA Ops:
  7.3 2.4 copy.29
  10.7 16.0 %all-gather = f32[256,128]{1,0:T(8,128)S(1)} all-gather(f32[16,128]{1,0:T(8,128)S(1)} %bitcast.25), channel_id=2, replica_groups=mesh['dp'=2,'expert'=16] {'expert'}, dimensions={0}, use_global_device_ids=true | all-gather | bytes 139264 | tf_op jit(solution)/shard_map/all_gather | solution.py:170
  26.7 19.7 %all-gather.6.cloned.1.call-done = bf16[1024,1152]{0,1:T(8,128)(2,1)} async-done(((bf16[512,1152]{0,1:T(8,128)(2,1)}), bf16[1024,1152]{0,1:T(8,128)(2,1)}) %all-gather.6.cloned.1.call-update) | async-done | bytes 2359312 | tf_op jit(solution)/shard_map/all_gather | solution.py:164
  46.4 77.5 %all-gather.4.cloned.1.call-done = bf16[2048,2048]{1,0:T(8,128)(2,1)} async-done(((bf16[128,2048]{1,0:T(8,128)(2,1)}), bf16[2048,2048]{1,0:T(8,128)(2,1)}) %all-gather.4.cloned.1.call-update) | async-done | bytes 8388624 | tf_op jit(solution)/shard_map/all_gather | solution.py:166
  123.9 5.9 %fusion.2 = f32[2048,768]{0,1:T(8,128)S(1)} fusion(bf16[2048,2048]{1,0:T(8,128)(2,1)} %all-gather.4.cloned.1.call-done, bf16[1024,1152]{0,1:T(8,128)(2,1)} %all-gather.6.cloned.1.call-done), kind=kOutput, calls=%fused_computation.8 | convolution fusion | flops 3221225472 | bytes 12058624 | tf_op jit(solution)/shard_map/dot_general | solution.py:175
  129.8 4.7 %multiply_convert_fusion.3 = (bf16[2048,384]{0,1:T(8,128)(2,1)S(1)}, bf16[2048,384]{0,1:T(8,128)(2,1)S(1)}, bf16[2048,384]{0,1:T(8,128)(2,1)S(1)}) fusion(f32[2048,768]{0,1:T(8,128)S(1)} %fusion.2, bf16[1024,1152]{0,1:T(8,128)(2,1)} %all-gather.6.cloned.1.call-done, bf16[2048,2048]{1,0:T(8,128)(2,1)S(1)} %copy-done.8, f32[2048]{0:T(1024)S(1)} %bitcast.26), kind=kOutput, calls=%fused_computation.13 | convolution fusion | flops 1628700672 | bytes 15998976 | tf_op jit(solution)/shard_map/dot_general | solution.py:186
  136.8 3.4 fusion.10
  148.9 26.2 %reduce-scatter.8.cloned.1.call-done = bf16[512,1152]{0,1:T(8,128)(2,1)} async-done(((bf16[1024,1152]{0,1:T(8,128)(2,1)}), bf16[512,1152]{0,1:T(8,128)(2,1)}) %reduce-scatter.8.cloned.1.call-update) | async-done | bytes 1179664 | tf_op jit(solution)/shard_map/reduce_scatter | solution.py:193
  175.1 5.8 %fusion.16 = (bf16[512,1152]{0,1:T(8,128)(2,1)S(1)}, bf16[512,1152]{0,1:T(8,128)(2,1)}, bf16[512,1152]{0,1:T(8,128)(2,1)S(1)}) fusion(bf16[512,1152]{0,1:T(8,128)(2,1)} %reduce-scatter.8.cloned.1.call-done, f32[1,512,3,384]{1,3,2,0:T(8,128)} %copy.31, f32[1,512,3,384]{1,3,2,0:T(8,128)} %copy.30, bf16[1,512,3,384]{1,3,2,0:T(8,128)(2,1)S(1)} %copy-done), kind=kLoop, calls=%fused_computation.33 | loop fusion | flops 10616832 | bytes 10616832 | tf_op jit(solution)/shard_map/convert_element_type | solution.py:202
  181.0 2.4 copy.32
  183.3 6.4 %all-to-all-start = ((bf16[16,32,1152]{2,1,0:T(8,128)(2,1)}), bf16[16,32,1152]{2,1,0:T(8,128)(2,1)S(1)}, u32[]{:S(2)}, u32[]{:S(2)}) async-start(bf16[16,32,1152]{2,1,0:T(8,128)(2,1)} %bitcast.6), calls=%async_computation.3 | async-start | bytes 2359296 | tf_op jit(solution)/shard_map/all_to_all | solution.py:203
  189.8 7.8 %convolution_convert_fusion = bf16[2048,1024]{1,0:T(8,128)(2,1)} fusion(bf16[2048,384]{0,1:T(8,128)(2,1)} %copy-done.12, bf16[2048,384]{0,1:T(8,128)(2,1)} %copy-done.11, bf16[1024,1152]{0,1:T(8,128)(2,1)} %all-gather.6.cloned.1.call-done), kind=kOutput, calls=%fused_computation.5 | convolution fusion | flops 3229614080 | bytes 8912896 | tf_op jit(solution)/shard_map/dot_general | solution.py:194
  199.0 18.5 %all-to-all-done = bf16[16,32,1152]{2,1,0:T(8,128)(2,1)S(1)} async-done(((bf16[16,32,1152]{2,1,0:T(8,128)(2,1)}), bf16[16,32,1152]{2,1,0:T(8,128)(2,1)S(1)}, u32[]{:S(2)}, u32[]{:S(2)}) %all-to-all-start) | async-done | bytes 1179680 | tf_op jit(solution)/shard_map/all_to_all | solution.py:203
  217.5 4.9 %all-to-all-start.2 = ((bf16[16,32,1152]{2,1,0:T(8,128)(2,1)}), bf16[16,32,1152]{2,1,0:T(8,128)(2,1)S(1)}, u32[]{:S(2)}, u32[]{:S(2)}) async-start(bf16[16,32,1152]{2,1,0:T(8,128)(2,1)} %bitcast.7), calls=%async_computation.5 | async-start | bytes 2359296 | tf_op jit(solution)/shard_map/all_to_all | solution.py:203
  223.8 43.1 %all-to-all-done.2 = bf16[16,32,1152]{2,1,0:T(8,128)(2,1)S(1)} async-done(((bf16[16,32,1152]{2,1,0:T(8,128)(2,1)}), bf16[16,32,1152]{2,1,0:T(8,128)(2,1)S(1)}, u32[]{:S(2)}, u32[]{:S(2)}) %all-to-all-start.2) | async-done | bytes 1179680 | tf_op jit(solution)/shard_map/all_to_all | solution.py:203
  266.9 4.9 %all-to-all-start.4 = ((bf16[16,32,1152]{2,1,0:T(8,128)(2,1)}), bf16[16,32,1152]{2,1,0:T(8,128)(2,1)S(1)}, u32[]{:S(2)}, u32[]{:S(2)}) async-start(bf16[16,32,1152]{2,1,0:T(8,128)(2,1)} %bitcast.23), calls=%async_computation.7 | async-start | bytes 2359296 | tf_op jit(solution)/shard_map/all_to_all | solution.py:203
  273.5 33.8 %all-to-all-done.4 = bf16[16,32,1152]{2,1,0:T(8,128)(2,1)S(1)} async-done(((bf16[16,32,1152]{2,1,0:T(8,128)(2,1)}), bf16[16,32,1152]{2,1,0:T(8,128)(2,1)S(1)}, u32[]{:S(2)}, u32[]{:S(2)}) %all-to-all-start.4) | async-done | bytes 1179680 | tf_op jit(solution)/shard_map/all_to_all | solution.py:203
  307.2 5.1 %all-to-all-start.1 = ((bf16[16,32,1152]{2,1,0:T(8,128)(2,1)}), bf16[16,32,1152]{2,1,0:T(8,128)(2,1)S(1)}, u32[]{:S(2)}, u32[]{:S(2)}) async-start(bf16[16,32,1152]{2,1,0:T(8,128)(2,1)} %gather_fusion), calls=%async_computation.4 | async-start | bytes 2359296 | tf_op jit(solution)/shard_map/all_to_all | solution.py:204
  312.4 6.0 %multiply_convert_fusion.1 = bf16[2048,1024]{1,0:T(8,128)(2,1)} fusion(bf16[2048,384]{0,1:T(8,128)(2,1)} %copy-done.10, f32[2048]{0:T(1024)S(1)} %bitcast.28, bf16[1024,1152]{0,1:T(8,128)(2,1)} %all-gather.6.cloned.1.call-done), kind=kOutput, calls=%fused_computation.4 | convolution fusion | flops 1614807040 | bytes 6561792 | tf_op jit(solution)/shard_map/dot_general | solution.py:181
  320.1 20.0 %all-to-all-done.1 = bf16[16,32,1152]{2,1,0:T(8,128)(2,1)S(1)} async-done(((bf16[16,32,1152]{2,1,0:T(8,128)(2,1)}), bf16[16,32,1152]{2,1,0:T(8,128)(2,1)S(1)}, u32[]{:S(2)}, u32[]{:S(2)}) %all-to-all-start.1) | async-done | bytes 1179680 | tf_op jit(solution)/shard_map/all_to_all | solution.py:204
  340.1 4.9 %all-to-all-start.3 = ((bf16[16,32,1152]{2,1,0:T(8,128)(2,1)}), bf16[16,32,1152]{2,1,0:T(8,128)(2,1)}, u32[]{:S(2)}, u32[]{:S(2)}) async-start(bf16[16,32,1152]{2,1,0:T(8,128)(2,1)} %gather_fusion.1), calls=%async_computation.6 | async-start | bytes 2359296 | tf_op jit(solution)/shard_map/all_to_all | solution.py:204
  346.6 43.0 %all-to-all-done.3 = bf16[16,32,1152]{2,1,0:T(8,128)(2,1)} async-done(((bf16[16,32,1152]{2,1,0:T(8,128)(2,1)}), bf16[16,32,1152]{2,1,0:T(8,128)(2,1)}, u32[]{:S(2)}, u32[]{:S(2)}) %all-to-all-start.3) | async-done | bytes 1179680 | tf_op jit(solution)/shard_map/all_to_all | solution.py:204
  389.6 5.0 %all-to-all-start.5 = ((bf16[16,32,1152]{2,1,0:T(8,128)(2,1)}), bf16[16,32,1152]{2,1,0:T(8,128)(2,1)}, u32[]{:S(2)}, u32[]{:S(2)}) async-start(bf16[16,32,1152]{2,1,0:T(8,128)(2,1)} %gather_fusion.2), calls=%async_computation.8 | async-start | bytes 2359296 | tf_op jit(solution)/shard_map/all_to_all | solution.py:204
  399.6 30.4 %all-to-all-done.5 = bf16[16,32,1152]{2,1,0:T(8,128)(2,1)} async-done(((bf16[16,32,1152]{2,1,0:T(8,128)(2,1)}), bf16[16,32,1152]{2,1,0:T(8,128)(2,1)}, u32[]{:S(2)}, u32[]{:S(2)}) %all-to-all-start.5) | async-done | bytes 1179680 | tf_op jit(solution)/shard_map/all_to_all | solution.py:204
  (60 shorter events, 28.2 us)
Async XLA Ops:
  7.2 2.6 copy-start.5
  7.2 2.6 copy-start.4
  7.2 3.5 copy-start.7
  7.2 3.5 copy-start.6
  7.2 39.2 %all-gather.6.cloned.1.call-start = ((), (), s32[]{:S(2)}) async-start(), calls=%async_computation.10 | async-start | bytes 3538944 | tf_op jit(solution)/shard_map/all_gather | solution.py:164
  9.7 114.2 %all-gather.4.cloned.1.call-start = ((), (), s32[]{:S(2)}) async-start(), calls=%async_computation.9 | async-start | bytes 8912896 | tf_op jit(solution)/shard_map/all_gather | solution.py:166
  10.6 164.5 %reduce-scatter.8.cloned.1.call-start = ((), (), s32[]{:S(2)}) async-start(), calls=%async_computation.13 | async-start | bytes 3538944 | tf_op jit(solution)/shard_map/reduce_scatter | solution.py:193
  123.9 5.9 %copy-start.8 = (bf16[2048,2048]{1,0:T(8,128)(2,1)S(1)}, bf16[2048,2048]{1,0:T(8,128)(2,1)}, u32[]{:S(2)}) copy-start(bf16[2048,2048]{1,0:T(8,128)(2,1)} %all-gather.4.cloned.1.call-done) | copy-start | bytes 25165828
  134.6 2.0 copy-start.10
  134.6 2.0 copy-start.11
  134.6 2.2 copy-start.12
  141.8 1.3 copy-start.3
  146.9 28.2 %copy-start = (bf16[1,512,3,384]{1,3,2,0:T(8,128)(2,1)S(1)}, bf16[1,512,3,384]{1,3,2,0:T(8,128)(2,1)}, u32[]{:S(2)}) copy-start(bf16[1,512,3,384]{1,3,2,0:T(8,128)(2,1)} %copy.29) | copy-start | bytes 3538948
  183.3 34.1 %all-to-all-start = ((bf16[16,32,1152]{2,1,0:T(8,128)(2,1)}), bf16[16,32,1152]{2,1,0:T(8,128)(2,1)S(1)}, u32[]{:S(2)}, u32[]{:S(2)}) async-start(bf16[16,32,1152]{2,1,0:T(8,128)(2,1)} %bitcast.6), calls=%async_computation.3 | async-start | bytes 2359296 | tf_op jit(solution)/shard_map/all_to_all | solution.py:203
  189.7 243.7 %reduce-scatter.6.cloned.1.call-start = ((), (), s32[]{:S(2)}) async-start(), calls=%async_computation.12 | async-start | bytes 4456448 | tf_op jit(solution)/shard_map/reduce_scatter | solution.py:195
  217.5 49.4 %all-to-all-start.2 = ((bf16[16,32,1152]{2,1,0:T(8,128)(2,1)}), bf16[16,32,1152]{2,1,0:T(8,128)(2,1)S(1)}, u32[]{:S(2)}, u32[]{:S(2)}) async-start(bf16[16,32,1152]{2,1,0:T(8,128)(2,1)} %bitcast.7), calls=%async_computation.5 | async-start | bytes 2359296 | tf_op jit(solution)/shard_map/all_to_all | solution.py:203
  222.3 49.4 %copy-start.9 = (s32[16]{0:T(128)S(1)}, s32[16]{0:T(128)}, u32[]{:S(2)}) copy-start(s32[16]{0:T(128)} %param.12) | copy-start | bytes 196
  266.9 40.3 %all-to-all-start.4 = ((bf16[16,32,1152]{2,1,0:T(8,128)(2,1)}), bf16[16,32,1152]{2,1,0:T(8,128)(2,1)S(1)}, u32[]{:S(2)}, u32[]{:S(2)}) async-start(bf16[16,32,1152]{2,1,0:T(8,128)(2,1)} %bitcast.23), calls=%async_computation.7 | async-start | bytes 2359296 | tf_op jit(solution)/shard_map/all_to_all | solution.py:203
  307.2 32.8 %all-to-all-start.1 = ((bf16[16,32,1152]{2,1,0:T(8,128)(2,1)}), bf16[16,32,1152]{2,1,0:T(8,128)(2,1)S(1)}, u32[]{:S(2)}, u32[]{:S(2)}) async-start(bf16[16,32,1152]{2,1,0:T(8,128)(2,1)} %gather_fusion), calls=%async_computation.4 | async-start | bytes 2359296 | tf_op jit(solution)/shard_map/all_to_all | solution.py:204
  312.3 121.1 %reduce-scatter.4.cloned.1.call-start = ((), (), s32[]{:S(2)}) async-start(), calls=%async_computation.11 | async-start | bytes 4456448 | tf_op jit(solution)/shard_map/reduce_scatter | solution.py:182
  340.1 6.5 %copy-start.1 = (bf16[16,32,1152]{2,1,0:T(8,128)(2,1)}, bf16[16,32,1152]{2,1,0:T(8,128)(2,1)S(1)}, u32[]{:S(2)}) copy-start(bf16[16,32,1152]{2,1,0:T(8,128)(2,1)S(1)} %all-to-all-done.1) | copy-start | bytes 3538948
  340.1 49.5 %all-to-all-start.3 = ((bf16[16,32,1152]{2,1,0:T(8,128)(2,1)}), bf16[16,32,1152]{2,1,0:T(8,128)(2,1)}, u32[]{:S(2)}, u32[]{:S(2)}) async-start(bf16[16,32,1152]{2,1,0:T(8,128)(2,1)} %gather_fusion.1), calls=%async_computation.6 | async-start | bytes 2359296 | tf_op jit(solution)/shard_map/all_to_all | solution.py:204
  389.6 5.0 %copy-start.2 = (bf16[16,32,1152]{2,1,0:T(8,128)(2,1)S(1)}, bf16[16,32,1152]{2,1,0:T(8,128)(2,1)}, u32[]{:S(2)}) copy-start(bf16[16,32,1152]{2,1,0:T(8,128)(2,1)} %copy-done.1) | copy-start | bytes 3538948
  389.6 40.4 %all-to-all-start.5 = ((bf16[16,32,1152]{2,1,0:T(8,128)(2,1)}), bf16[16,32,1152]{2,1,0:T(8,128)(2,1)}, u32[]{:S(2)}, u32[]{:S(2)}) async-start(bf16[16,32,1152]{2,1,0:T(8,128)(2,1)} %gather_fusion.2), calls=%async_computation.8 | async-start | bytes 2359296 | tf_op jit(solution)/shard_map/all_to_all | solution.py:204
Sparse Core Ops, SparseCore 0:
  10.2 36.2 all-gather.5
  49.2 74.7 all-gather.3
  142.0 33.1 reduce-scatter.7
  197.7 95.5 reduce-scatter.5
  318.5 96.6 reduce-scatter.3
